TPU v7x, 512 devices: a whole 4x8x8 slice. The times are simulated.
512 devices in a mesh: dp: 8 (over y), ctx: 64 (over z, x, core).
Axes of the slice: x: 4, y: 8, z: 8, core: 2. Of those that a mesh axis runs over, the one named last changes fastest.
Arguments:
- queries: bfloat16 [8, 8192, 1024], P('dp', 'ctx'), may hold values from -6 to 6
- keys: bfloat16 [8, 8192, 1024], P('dp', 'ctx'), may hold values from -0.5390625 to 0.5390625
- values: bfloat16 [8, 8192, 1024], P('dp', 'ctx'), may hold values from -6 to 6
- gain: float32 [1024], replicated, may hold values from 0.1 to 1.9
- grad_out: bfloat16 [8, 8192, 1024], P('dp', 'ctx'), may hold values from -16 to 16
Outputs:
- output: bfloat16 [8, 8192, 1024], P('dp', 'ctx')
- grad_queries: bfloat16 [8, 8192, 1024], P('dp', 'ctx')
- grad_keys: bfloat16 [8, 8192, 1024], P('dp', 'ctx')
- grad_values: bfloat16 [8, 8192, 1024], P('dp', 'ctx')
- grad_gain: float32 [1024], replicated
All inputs are finite; a program needn't handle non-finite values.
Results may differ from a plain program's by a relative error of at most 0.006.
Values sent between devices are 32-bit elements; how exact they have to be, the bound alone decides.
No kernel may reach another device: no remote copies, remote signals or barrier semaphores. Data moves between devices by JAX's collectives and lax.ppermute only.
A program may use at most 128 MiB of HBM per device.

v0:
```python
import jax
import jax.numpy as jnp
from jax import lax
from jax.sharding import PartitionSpec as P

HEAD_DIM = 64
GROUP = 128


def entering(part, axis, combine, identity):
    place = lax.axis_index(axis)
    gathered = lax.all_gather(part, axis)
    state = jnp.zeros_like(part) + jnp.asarray(identity, part.dtype)

    def one(hop, state):
        return combine(state, lax.dynamic_index_in_dim(gathered, hop, 0, False))

    return lax.fori_loop(0, place, one, state)


def add_states(earlier, later_one):
    return earlier + later_one


def per_device(queries, keys, values, gain, grad_out):
    rows = queries.shape[1]
    width = queries.shape[2]
    heads = width // HEAD_DIM
    blocks = rows // GROUP
    shape4 = (blocks, GROUP, heads, HEAD_DIM)
    query_rows = queries.reshape(shape4)
    key_rows = keys.reshape(shape4)
    value_rows = values.reshape(shape4)
    f32 = jnp.float32
    block_kv = jnp.einsum("nrhd,nrhe->nhde", key_rows, value_rows, preferred_element_type=f32)
    local_kv = jnp.sum(block_kv, 0)
    empty_state = jnp.zeros((heads, HEAD_DIM, HEAD_DIM), f32)
    carried = entering(local_kv, "ctx", add_states, empty_state)
    state = carried[None] + (jnp.cumsum(block_kv, 0) - block_kv)
    state_low = state.astype(jnp.bfloat16)
    causal = jnp.tril(jnp.ones((GROUP, GROUP), bool))
    scores = jnp.where(
        causal[None, None],
        jnp.einsum("nthd,nshd->nhts", query_rows, key_rows, preferred_element_type=f32),
        0.0,
    ).astype(jnp.bfloat16)
    attn = jnp.einsum("nhts,nshe->nthe", scores, value_rows, preferred_element_type=f32)
    attn = attn + jnp.einsum("nthd,nhde->nthe", query_rows, state_low, preferred_element_type=f32)
    attn = attn.reshape(rows, width)
    inverse_rms = lax.rsqrt(jnp.mean(attn * attn, -1, keepdims=True) + 1e-06)
    normed = attn * inverse_rms
    output = (normed * gain).astype(jnp.bfloat16)
    grad_f = grad_out[0].astype(f32)
    gain_part = jnp.sum(grad_f * normed, 0)
    grad_norm = grad_f * gain
    grad_attn = (
        inverse_rms * (grad_norm - normed * jnp.mean(grad_norm * normed, -1, keepdims=True))
    ).astype(jnp.bfloat16)
    grad_attn = grad_attn.reshape(shape4)
    block_adjoint = jnp.einsum("nthd,nthe->nhde", query_rows, grad_attn, preferred_element_type=f32)
    local_adjoint = jnp.sum(block_adjoint, 0)
    dscores = jnp.where(
        causal[None, None],
        jnp.einsum("nthe,nshe->nhts", grad_attn, value_rows, preferred_element_type=f32),
        0.0,
    ).astype(jnp.bfloat16)
    grad_queries = jnp.einsum("nhts,nshd->nthd", dscores, key_rows, preferred_element_type=f32)
    grad_queries = grad_queries + jnp.einsum(
        "nthe,nhde->nthd", grad_attn, state_low, preferred_element_type=f32
    )
    grad_keys = jnp.einsum("nhts,nthd->nshd", dscores, query_rows, preferred_element_type=f32)
    grad_values = jnp.einsum("nhts,nthe->nshe", scores, grad_attn, preferred_element_type=f32)
    total, gain_ctx = lax.psum((local_adjoint, gain_part), "ctx")
    before = entering(local_adjoint, "ctx", add_states, empty_state)
    from_later = total - before - local_adjoint
    grad_gain = lax.psum(gain_ctx, "dp")
    from_end = jnp.cumsum(block_adjoint[::-1], 0)[::-1]
    later = from_later[None] + (from_end - block_adjoint)
    later_low = later.astype(jnp.bfloat16)
    grad_keys = grad_keys + jnp.einsum(
        "nshe,nhde->nshd", value_rows, later_low, preferred_element_type=f32
    )
    grad_values = grad_values + jnp.einsum(
        "nshd,nhde->nshe", key_rows, later_low, preferred_element_type=f32
    )
    flat = (1, rows, width)
    return (
        output.reshape(flat),
        grad_queries.reshape(flat).astype(jnp.bfloat16),
        grad_keys.reshape(flat).astype(jnp.bfloat16),
        grad_values.reshape(flat).astype(jnp.bfloat16),
        grad_gain,
    )


def solution(mesh):
    return jax.shard_map(
        per_device,
        mesh=mesh,
        in_specs=(
            P("dp", "ctx", None),
            P("dp", "ctx", None),
            P("dp", "ctx", None),
            P(),
            P("dp", "ctx", None),
        ),
        out_specs=(
            P("dp", "ctx", None),
            P("dp", "ctx", None),
            P("dp", "ctx", None),
            P("dp", "ctx", None),
            P(),
        ),
        check_vma=False,
    )
```

profile of v0, /device:TPU:8, one launch (start us, length us, event | category | flops | bytes accessed | tf_op | source)
XLA Modules:
  0.0 591.7 jit_solution(8018616743634753172)
XLA Ops:
  7.2 0.0 all-gather.5.cloned.1.call-start
  7.2 1.1 copy.48
  8.3 1.1 copy.49
  9.5 1.1 fusion.22
  10.5 0.0 all-gather.5.cloned.1.call-update
  10.6 0.0 all-gather.7.cloned.1.call-start
  10.6 0.8 mul.110
  11.4 1.1 copy.47
  12.5 1.1 copy.52
  13.6 0.4 fusion
  14.0 0.4 convolution_bitcast_fusion.3
  14.4 150.3 %all-gather.5.cloned.1.call-done = f32[1024,64,64]{2,1,0:T(8,128)} async-done(((f32[16,64,64]{2,1,0:T(8,128)}), f32[1024,64,64]{2,1,0:T(8,128)}) %all-gather.5.cloned.1.call-update) | async-done | bytes 16777232 | tf_op jit(solution)/shard_map/all_gather | solution.py:12
  164.7 1.1 add_convert_fusion.1
  165.9 0.3 fusion.16
  166.2 0.2 copy.53
  166.4 1.2 fusion.11
  167.6 0.3 convolution_bitcast_fusion.1
  168.0 0.0 copy-start
  168.0 1.0 copy.55
  169.0 0.0 all-gather.7.cloned.1.call-update
  169.0 0.0 all-reduce.2.cloned.1.call-start
  169.1 1.0 copy.51
  170.1 0.2 fusion.17
  170.3 0.4 fusion.1
  170.6 0.4 convolution_bitcast_fusion.2
  171.1 0.9 fusion.2
  172.0 1.8 copy.58
  173.8 203.0 %psum.22 = f32[1024]{0:T(1024)S(1)} all-reduce(f32[1024]{0:T(1024)S(1)} %get-tuple-element.76), channel_id=1, replica_groups=mesh['dp'=8,'ctx'=64] {'ctx'}, use_global_device_ids=true, to_apply=%region_8.9 | all-reduce | flops 1024 | bytes 8192 | tf_op jit(solution)/shard_map/psum | solution.py:73
  376.8 16.3 %psum.23 = f32[1024]{0:T(1024)} all-reduce(f32[1024]{0:T(1024)S(1)} %psum.22), channel_id=1, replica_groups=mesh['dp'=8,'ctx'=64] {'dp'}, use_global_device_ids=true, to_apply=%region_9.10 | all-reduce | flops 1024 | bytes 8192 | tf_op jit(solution)/shard_map/psum | solution.py:76
  393.1 1.9 multiply_convert_fusion
  395.0 0.3 fusion.23
  395.3 0.3 convolution_bitcast_fusion
  395.5 0.0 copy-done
  395.6 0.0 all-reduce.2.cloned.1.call-update
  395.6 0.0 all-gather.7.cloned.1.call-done
  395.7 0.2 copy.56
  395.9 185.8 %all-reduce.2.cloned.1.call-done = f32[16,64,64]{1,2,0:T(8,128)} async-done(((f32[16,64,64]{1,2,0:T(8,128)}), f32[16,64,64]{1,2,0:T(8,128)}) %all-reduce.2.cloned.1.call-update) | async-done | bytes 262160 | tf_op jit(solution)/shard_map/psum | solution.py:73
  581.6 1.3 add_convert_fusion
  583.0 0.2 fusion.4
  583.2 0.3 fusion.3
  583.5 0.8 copy.59
  584.3 0.8 copy.60
  (7 shorter events, 0.1 us)
Async XLA Ops:
  7.2 157.5 %all-gather.5.cloned.1.call-start = ((), (), s32[]{:S(2)}) async-start(), calls=%async_computation.1 | async-start | bytes 34078720 | tf_op jit(solution)/shard_map/all_gather | solution.py:12
  10.6 385.0 %all-gather.7.cloned.1.call-start = ((), (), s32[]{:S(2)}) async-start(), calls=%async_computation.2 | async-start | bytes 34078720 | tf_op jit(solution)/shard_map/all_gather | solution.py:12
  168.0 227.6 %copy-start = (f32[16,64,64]{1,2,0:T(8,128)}, f32[16,64,64]{1,2,0:T(8,128)S(1)}, u32[]{:S(2)}) copy-start(f32[16,64,64]{1,2,0:T(8,128)S(1)} %convolution_bitcast_fusion.1) | copy-start | bytes 786436
  169.0 412.6 %all-reduce.2.cloned.1.call-start = ((), (), s32[]{:S(2)}) async-start(), calls=%async_computation | async-start | bytes 1048576 | tf_op jit(solution)/shard_map/psum | solution.py:73
Sparse Core Ops, SparseCore 0:
  11.4 153.2 all-gather.4
  169.1 219.1 all-gather.6
  395.7 185.8 all-reduce.1
where the time goes:
time: 598 us; the launch traced here: 592 us
  waiting for transfers between devices  336 us (56%)
  blocking collectives  219 us (37%)
  between operations  13.9 us (2%)
  local copies, waits for them, and re-layouts  11.2 us (2%)
    psum x1, blocking collectives, per_device(): total, gain_ctx = lax.psum((local_adjoint, gain_part), 'ctx')  203 us
    psum x1, waiting for transfers between devices, per_device(): total, gain_ctx = lax.psum((local_adjoint, gain_part), 'ctx')  186 us
    all_gather x2, waiting for transfers between devices, entering(): gathered = lax.all_gather(part, axis)  150 us
    psum x1, blocking collectives, per_device(): grad_gain = lax.psum(gain_ctx, 'dp')  16.3 us
  transfers between devices with their start and end apart: 3, of which 2 were waited for; matrix products, arithmetic and copies ran while one was open for 2% of the time, Pallas kernels for 0%

commit v1 on v0

--- a/solution.py
+++ b/solution.py
@@ -73,7 +73,11 @@
     total, gain_ctx = lax.psum((local_adjoint, gain_part), "ctx")
     before = entering(local_adjoint, "ctx", add_states, empty_state)
     from_later = total - before - local_adjoint
-    grad_gain = lax.psum(gain_ctx, "dp")
+    grad_gain = gain_ctx
+    for hop_ in (1, 2, 4):
+        grad_gain = grad_gain + lax.ppermute(
+            grad_gain, "dp", [(dev, dev ^ hop_) for dev in range(8)]
+        )
     from_end = jnp.cumsum(block_adjoint[::-1], 0)[::-1]
     later = from_later[None] + (from_end - block_adjoint)
     later_low = later.astype(jnp.bfloat16)

time: 598 us -> 600 us (level)
  blocking collectives: 219 us -> 203 us
  starting transfers between devices: 0.12 us -> 13.6 us
    psum x1 -> x0, blocking collectives: 16.3 us -> none  [per_device(): grad_gain = lax.psum(gain_ctx, 'dp')]
    ppermute x0 -> x3, starting transfers between devices: none -> 13.4 us  [per_device(): lax.ppermute(grad_gain, 'dp', [(dev, dev ^ hop_) for dev in range(8)])]
  transfers between devices with their start and end apart: 3 -> 6, of which waited for: 2 -> 5; matrix products, arithmetic and copies ran while one was open for 2% -> 2% of each run, Pallas kernels for 0% -> 0%
where the time goes in v1:
time: 600 us; the launch traced here: 593 us
  waiting for transfers between devices  339 us (56%)
  blocking collectives  203 us (34%)
  between operations  13.9 us (2%)
  starting transfers between devices  13.6 us (2%)
  local copies, waits for them, and re-layouts  9.43 us (2%)
  matrix products  8.31 us (1%)
    psum x1, blocking collectives, per_device(): total, gain_ctx = lax.psum((local_adjoint, gain_part), 'ctx')  203 us
    psum x1, waiting for transfers between devices, per_device(): total, gain_ctx = lax.psum((local_adjoint, gain_part), 'ctx')  187 us
    all_gather x2, waiting for transfers between devices, entering(): gathered = lax.all_gather(part, axis)  149 us
    ppermute x3, starting transfers between devices, per_device(): lax.ppermute(grad_gain, 'dp', [(dev, dev ^ hop_) for dev in range(8)])  13.4 us
  transfers between devices with their start and end apart: 6, of which 5 were waited for; matrix products, arithmetic and copies ran while one was open for 2% of the time, Pallas kernels for 0%

profile of v1, /device:TPU:8, one launch (start us, length us, event | category | flops | bytes accessed | tf_op | source)
XLA Modules:
  0.0 593.4 jit_solution(17233709543423744756)
XLA Ops:
  7.2 0.0 all-gather.5.cloned.1.call-start
  7.2 1.1 copy.48
  8.3 1.1 copy.49
  9.5 1.1 fusion.22
  10.5 0.0 all-gather.5.cloned.1.call-update
  10.6 0.0 all-gather.7.cloned.1.call-start
  10.6 0.8 mul.110
  11.4 1.1 copy.47
  12.5 1.1 copy.52
  13.6 0.4 fusion
  14.0 1.3 convolution_bitcast_fusion.3
  15.2 149.4 %all-gather.5.cloned.1.call-done = f32[1024,64,64]{2,1,0:T(8,128)} async-done(((f32[16,64,64]{2,1,0:T(8,128)}), f32[1024,64,64]{2,1,0:T(8,128)}) %all-gather.5.cloned.1.call-update) | async-done | bytes 16777232 | tf_op jit(solution)/shard_map/all_gather | solution.py:12
  164.7 1.1 add_convert_fusion.1
  165.9 1.4 fusion.16
  167.3 0.2 copy.53
  167.5 1.2 fusion.11
  168.7 0.3 convolution_bitcast_fusion.1
  169.0 0.0 copy-start
  169.0 1.0 copy.55
  170.0 0.0 all-gather.7.cloned.1.call-update
  170.1 0.0 all-reduce.2.cloned.1.call-start
  170.1 203.2 %psum.15 = f32[1024]{0:T(1024)S(1)} all-reduce(f32[1024]{0:T(1024)S(1)} %get-tuple-element.76), channel_id=1, replica_groups=mesh['dp'=8,'ctx'=64] {'ctx'}, use_global_device_ids=true, to_apply=%region_8.9 | all-reduce | flops 1024 | bytes 8192 | tf_op jit(solution)/shard_map/psum | solution.py:73
  373.3 2.4 collective-permute-start
  375.7 0.2 fusion.17
  375.9 0.4 fusion.1
  376.3 1.1 fusion.23
  377.4 0.3 convolution_bitcast_fusion
  377.6 0.5 convolution_bitcast_fusion.2
  378.1 0.7 collective-permute-done
  378.8 4.3 collective-permute-start.1
  383.1 0.2 fusion.2
  383.3 0.2 copy.51
  383.5 1.6 collective-permute-done.1
  385.1 6.7 %collective-permute-start.2 = (f32[1024]{0:T(1024)S(1)}, f32[1024]{0:T(1024)S(1)}, u32[]{:S(2)}, u32[]{:S(2)}) collective-permute-start(f32[1024]{0:T(1024)S(1)} %add.90), channel_id=1, source_target_pairs={{0,256},{64,320},{128,384},{192,448},{256,0},{320,64},{384,128},{4... | collective-permute-start | bytes 12296 | tf_op jit(solution)/shard_map/ppermute | solution.py:78
  391.9 1.5 multiply_convert_fusion
  393.4 0.8 copy.58
  394.2 0.0 copy-done
  394.2 0.0 all-reduce.2.cloned.1.call-update
  394.2 0.3 collective-permute-done.2
  394.5 0.6 add.91
  395.1 0.0 all-gather.7.cloned.1.call-done
  395.2 0.2 copy.56
  395.4 186.9 %all-reduce.2.cloned.1.call-done = f32[16,64,64]{1,2,0:T(8,128)} async-done(((f32[16,64,64]{1,2,0:T(8,128)}), f32[16,64,64]{1,2,0:T(8,128)}) %all-reduce.2.cloned.1.call-update) | async-done | bytes 262160 | tf_op jit(solution)/shard_map/psum | solution.py:73
  582.3 1.3 add_convert_fusion
  583.6 1.3 fusion.4
  584.9 0.3 fusion.3
  585.1 0.8 copy.59
  586.0 0.8 copy.60
  (9 shorter events, 0.1 us)
Async XLA Ops:
  7.2 157.5 %all-gather.5.cloned.1.call-start = ((), (), s32[]{:S(2)}) async-start(), calls=%async_computation.1 | async-start | bytes 34078720 | tf_op jit(solution)/shard_map/all_gather | solution.py:12
  10.6 384.6 %all-gather.7.cloned.1.call-start = ((), (), s32[]{:S(2)}) async-start(), calls=%async_computation.2 | async-start | bytes 34078720 | tf_op jit(solution)/shard_map/all_gather | solution.py:12
  169.0 225.2 %copy-start = (f32[16,64,64]{1,2,0:T(8,128)}, f32[16,64,64]{1,2,0:T(8,128)S(1)}, u32[]{:S(2)}) copy-start(f32[16,64,64]{1,2,0:T(8,128)S(1)} %convolution_bitcast_fusion.1) | copy-start | bytes 786436
  170.1 412.2 %all-reduce.2.cloned.1.call-start = ((), (), s32[]{:S(2)}) async-start(), calls=%async_computation | async-start | bytes 1048576 | tf_op jit(solution)/shard_map/psum | solution.py:73
  373.3 5.5 collective-permute-start
  378.8 6.4 %collective-permute-start.1 = (f32[1024]{0:T(1024)S(1)}, f32[1024]{0:T(1024)S(1)}, u32[]{:S(2)}, u32[]{:S(2)}) collective-permute-start(f32[1024]{0:T(1024)S(1)} %add.89), channel_id=1, source_target_pairs={{0,128},{64,192},{128,0},{192,64},{256,384},{320,448},{384,256},{4... | collective-permute-start | bytes 12296 | tf_op jit(solution)/shard_map/ppermute | solution.py:78
  385.1 9.4 %collective-permute-start.2 = (f32[1024]{0:T(1024)S(1)}, f32[1024]{0:T(1024)S(1)}, u32[]{:S(2)}, u32[]{:S(2)}) collective-permute-start(f32[1024]{0:T(1024)S(1)} %add.90), channel_id=1, source_target_pairs={{0,256},{64,320},{128,384},{192,448},{256,0},{320,64},{384,128},{4... | collective-permute-start | bytes 12296 | tf_op jit(solution)/shard_map/ppermute | solution.py:78
Sparse Core Ops, SparseCore 0:
  11.4 153.2 all-gather.4
  170.2 219.0 all-gather.6
  394.4 187.8 all-reduce.1
